TPU v7x, 32 devices: a whole 2x2x4 slice. The times are simulated.
32 devices in a mesh: rep: 2 (over y), seq: 8 (over z, x), sub: 2 (over core).
Axes of the slice: x: 2, y: 2, z: 4, core: 2. Of those that a mesh axis runs over, the one named last changes fastest.
Arguments:
- lin_query: bfloat16 [2048, 2048], P(('rep', 'seq'), 'sub'), parts along dimension 0, may hold values from -6 to 6
- lin_key: bfloat16 [2048, 2048], P(('rep', 'seq'), 'sub'), parts along dimension 0, may hold values from -0.59765625 to 0.59765625
- lin_value: bfloat16 [2048, 2048], P(('rep', 'seq'), 'sub'), parts along dimension 0, may hold values from -6 to 6
- forget_log: float32 [2048, 16], P(('rep', 'seq'), 'sub'), parts along dimension 0, may hold values from -0.95 to 0
- norm_gain: float32 [2048], P('sub'), may hold values from 0.1 to 1.9
- soft_query: bfloat16 [2048, 2048], P(('rep', 'seq'), 'sub'), parts along dimension 0, may hold values from -34 to 34
- soft_key: bfloat16 [2048, 256], P(('rep', 'seq'), 'sub'), parts along dimension 0, may hold values from -6 to 6
- soft_value: bfloat16 [2048, 256], P(('rep', 'seq'), 'sub'), parts along dimension 0, may hold values from -6 to 6
- doc_lengths: int32 [2, 4], P('rep'), parts along dimension 0, may hold values from 1 to 512, 1024 in all within a row
Outputs:
- lin_out: bfloat16 [2048, 2048], P(('rep', 'seq'), 'sub'), parts along dimension 0
- soft_out: bfloat16 [2048, 2048], P(('rep', 'seq'), 'sub'), parts along dimension 0
There are 2 independent parts, one for each index of `rep`. A program takes and returns all parts, laid end to end along the dimension named above; an argument that names none is the same for every part. Nothing has to cross between parts.
Inputs may be any that keep to these rules, and one draw needn't show every extreme that they name: `doc_lengths`: each row holds the lengths of one sequence's 4 documents in order; a row sums to 1024.
All inputs are finite; a program needn't handle non-finite values.
Results may differ from a plain program's by a relative error of at most 0.0075.
Values may be sent and summed in bfloat16 or wider, within the bound.
A program may use at most 192 MiB of HBM per device.

v0:
```python
import math

import jax
import jax.numpy as jnp
from jax import lax
from jax.sharding import PartitionSpec as P

HEAD_DIM = 128


NEGATIVE = -1e30


def entering(array, axis, combine, identity):
    size, mine = (lax.axis_size(axis), lax.axis_index(axis))
    everything = jax.tree.map(
        lambda part, kind: lax.all_gather(part.astype(kind), axis),
        array,
        (jnp.bfloat16, jnp.bfloat16),
    )
    start = jax.tree.map(
        lambda part, zero: jnp.broadcast_to(jnp.asarray(zero, part.dtype), part.shape),
        array,
        identity,
    )

    def step(k, before):
        reached = k < mine
        new = combine(
            before, jax.tree.map(lambda part, own: part[k].astype(own.dtype), everything, array)
        )
        return jax.tree.map(lambda a, b: jnp.where(reached, a, b), new, before)

    return lax.fori_loop(0, size, step, start)


def passed_along(block, axis, distance):
    devices = range(lax.axis_size(axis))
    route = [(i - distance, i) for i in devices if i - distance in devices]
    return lax.ppermute(block, axis, route)


def document_ids(lengths_row, where_at):
    starts = jnp.cumsum(lengths_row) - lengths_row
    ids = jnp.sum((starts[None, :] <= where_at[:, None]).astype(jnp.int32), axis=1) - 1
    begins = jnp.any(starts[None, :] == where_at[:, None], axis=1)
    return (ids, begins)


def linear_parts(lin_query, lin_key, lin_value, forget_log, ids, begins):
    rows_here, heads_here = forget_log.shape
    queries = lin_query.reshape(rows_here, heads_here, HEAD_DIM)
    keys = lin_key.reshape(rows_here, heads_here, HEAD_DIM)
    values = lin_value.reshape(rows_here, heads_here, HEAD_DIM)
    cum = jnp.cumsum(forget_log, axis=0)
    live = (jnp.cumsum(begins.astype(jnp.int32)) == 0).astype(jnp.float32)
    order = jnp.arange(rows_here, dtype=jnp.int32)
    mask = (ids[:, None] == ids[None, :]) & (order[None, :] <= order[:, None])
    diff = cum.T[:, :, None] - cum.T[:, None, :]
    decay = jnp.where(mask[None], jnp.exp(jnp.where(mask[None], diff, 0.0)), 0.0)
    scores = jnp.einsum("thd,shd->hts", queries, keys, preferred_element_type=jnp.float32)
    weights = (scores * decay).astype(jnp.bfloat16)
    intra = jnp.einsum("hts,shd->thd", weights, values, preferred_element_type=jnp.float32)
    tail_mask = ids == ids[-1]
    tail = jnp.where(
        tail_mask[:, None], jnp.exp(jnp.where(tail_mask[:, None], cum[-1][None, :] - cum, 0.0)), 0.0
    )
    keyed = (keys * tail[:, :, None]).astype(jnp.bfloat16)
    local_state = jnp.einsum("shd,she->hde", keyed, values, preferred_element_type=jnp.float32)
    block_decay = jnp.exp(cum[-1]) * live[-1]
    queried = (queries * (jnp.exp(cum) * live[:, None])[:, :, None]).astype(jnp.bfloat16)
    return (intra, queried, local_state, block_decay)


def linear_finish(intra, queried, incoming, norm_gain):
    rows_here, heads_here, width = intra.shape
    inter = jnp.einsum(
        "thd,hde->the", queried, incoming.astype(jnp.bfloat16), preferred_element_type=jnp.float32
    )
    summed = intra + inter
    mean_square = jnp.mean(summed * summed, axis=-1, keepdims=True)
    normed = summed * lax.rsqrt(mean_square + 1e-06) * norm_gain.reshape(heads_here, width)
    return normed.reshape(rows_here, heads_here * width).astype(jnp.bfloat16)


def attend(running, queries, key_block, value_block, mask):
    peak, total, accum = running
    width = queries.shape[-1]
    scores = jnp.einsum(
        "tkgd,skd->kgts", queries, key_block, preferred_element_type=jnp.float32
    ) * (1.0 / math.sqrt(width))
    scores = jnp.where(mask, scores, NEGATIVE)
    new_peak = jnp.maximum(peak, jnp.max(scores, axis=-1))
    weights = jnp.where(mask, jnp.exp(scores - new_peak[..., None]), 0.0)
    rescale = jnp.exp(peak - new_peak)
    total = total * rescale + jnp.sum(weights, axis=-1)
    accum = accum * rescale[..., None] + jnp.einsum(
        "kgts,skd->kgtd",
        weights.astype(jnp.bfloat16),
        value_block,
        preferred_element_type=jnp.float32,
    )
    return (new_peak, total, accum)


def start_running(kv_here, group, count):
    return (
        jnp.full((kv_here, group, count), NEGATIVE, jnp.float32),
        jnp.zeros((kv_here, group, count), jnp.float32),
        jnp.zeros((kv_here, group, count, HEAD_DIM), jnp.float32),
    )


def finish_running(running, count, heads_here):
    peak, total, accum = running
    soft = (accum / total[..., None]).astype(jnp.bfloat16)
    return soft.transpose(2, 0, 1, 3).reshape(count, heads_here * HEAD_DIM)


def per_device(
    lin_query,
    lin_key,
    lin_value,
    forget_log,
    norm_gain,
    soft_query,
    soft_key,
    soft_value,
    doc_lengths,
):
    rows_here = lin_query.shape[0]
    seq_count = doc_lengths.shape[0]
    span = lax.axis_size("seq") // seq_count
    position = lax.axis_index("seq")
    rank = position % span
    lengths_row = doc_lengths[0]
    order = jnp.arange(rows_here, dtype=jnp.int32)
    query_where = rank * rows_here + order
    ids, begins = document_ids(lengths_row, query_where)
    intra, queried, local_state, block_decay = linear_parts(
        lin_query, lin_key, lin_value, forget_log, ids, begins
    )

    def combine_states(earlier, later):
        return (earlier[0] * later[0], later[0][:, None, None] * earlier[1] + later[1])

    identity = (jnp.ones_like(block_decay), jnp.zeros_like(local_state))
    scanned = entering((block_decay, local_state), "seq", combine_states, identity)
    lin_out = linear_finish(intra, queried, scanned[1], norm_gain)
    kv_here = soft_key.shape[1] // HEAD_DIM
    heads_here = soft_query.shape[1] // HEAD_DIM
    group = heads_here // kv_here
    queries = soft_query.reshape(rows_here, kv_here, group, HEAD_DIM)

    def piece_mask(start, count):
        key_where = start + jnp.arange(count, dtype=jnp.int32)
        source_ids, unused = document_ids(lengths_row, key_where)
        return (ids[:, None] == source_ids[None, :]) & (key_where[None, :] <= query_where[:, None])

    def attend_piece(running, key_piece, value_piece, start):
        count = key_piece.shape[0]
        key_block = key_piece.reshape(count, kv_here, HEAD_DIM)
        value_block = value_piece.reshape(count, kv_here, HEAD_DIM)
        return attend(running, queries, key_block, value_block, piece_mask(start, count))

    own_pair = jnp.stack([soft_key, soft_value])
    running = attend_piece(
        start_running(kv_here, group, rows_here), soft_key, soft_value, rank * rows_here
    )

    def visit_cycle(turn, state):
        moving, inner_state = state
        moving = passed_along(moving, "seq", 1)
        source = rank - turn - 1
        inner_state = lax.cond(
            source >= 0,
            lambda inner: attend_piece(inner, moving[0], moving[1], source * rows_here),
            lambda inner: inner,
            inner_state,
        )
        return (moving, inner_state)

    unused_pair, running = lax.fori_loop(0, span - 1, visit_cycle, (own_pair, running))
    soft_out = finish_running(running, rows_here, heads_here)
    return (lin_out, soft_out)


def solution(mesh):
    placed = (
        P(("rep", "seq"), "sub"),
        P(("rep", "seq"), "sub"),
        P(("rep", "seq"), "sub"),
        P(("rep", "seq"), "sub"),
        P("sub"),
        P(("rep", "seq"), "sub"),
        P(("rep", "seq"), "sub"),
        P(("rep", "seq"), "sub"),
        P("rep", None),
    )
    return jax.shard_map(
        per_device,
        mesh=mesh,
        in_specs=placed,
        out_specs=(P(("rep", "seq"), "sub"), P(("rep", "seq"), "sub")),
        check_vma=False,
    )
```

profile of v0, /device:TPU:20, one launch (start us, length us, event | category | flops | bytes accessed | tf_op | source)
XLA Modules:
  0.0 110.3 jit_solution(11577366015206899077)
XLA Ops:
  7.3 0.9 reduce-window_1_clone.1
  8.2 0.7 subtract_bitcast_fusion
  9.1 0.2 reduce-window.17
  9.4 0.8 copy.71
  10.2 0.5 slice.21
  10.7 0.7 slice.19
  11.4 0.7 broadcast_compare_fusion
  12.1 1.1 %copy.93 = bf16[128,1024]{0,1:T(8,128)(2,1)S(1)} copy(bf16[128,1024]{1,0:T(8,128)(2,1)} %param.16) | data formatting | bytes 524288 | tf_op jit(solution)/shard_map/reshape | solution.py:53
  13.2 0.2 reduce_window_sum.28
  13.4 0.7 slice_bitcast_fusion
  14.2 0.9 convolution_convert_fusion
  15.2 15.1 %all-gather.1 = bf16[8,1,8]{2,1,0:T(2,128)(2,1)S(1)} all-gather(bf16[1,1,8]{2,1,0:T(2,128)(2,1)S(1)} %get-tuple-element.517), channel_id=1, replica_groups=mesh['rep'=2,'seq'=8,'sub'=2] {'seq'}, dimensions={0}, use_global_device_ids=true | all-gather | bytes 144 | tf_op jit(solution)/shard_map/all_gather | solution.py:17
  30.4 0.1 compare_and_fusion.1
  30.6 0.2 copy.85
  30.8 0.2 copy.86
  31.0 0.2 fusion.65
  31.4 0.3 fusion.20
  31.7 59.4 %while.36 = (s32[]{:T(128)}, bf16[2,128,128]{2,1,0:T(8,128)(2,1)S(1)}, f32[1,8,128]{2,1,0:T(8,128)S(1)}, f32[1,8,128]{2,1,0:T(8,128)S(1)}, f32[1,8,128,128]{3,2,...) while((s32[]{:T(128)}, ...), condition=%wide.region_17.18_spmd.clone, body=%wide.region_10.17_spmd.clone.sunk | while | flops 68604696 | bytes 3480019 | solution.py:183
  31.8 2.6 %collective-permute-start = (bf16[2,128,128]{2,1,0:T(8,128)(2,1)S(1)}, bf16[2,128,128]{2,1,0:T(8,128)(2,1)S(1)}, u32[]{:S(2)}, u32[]{:S(2)}) collective-permute-start(bf16[2,128,128]{2,1,0:T(8,128)(2,1)S(1)} %get-tuple-element.666), channel_id=1, source_target_pairs={{0,2},{2,4},{4,6},{6,8},{8,10},{10,12},{12,14},{1,3},{3,5},{5,7},{... | collective-permute-start | bytes 196616 | tf_op jit(solution)/shard_map/while/body/eval_jaxpr/ppermute | solution.py:40
  34.4 4.6 %collective-permute-done = bf16[2,128,128]{2,1,0:T(8,128)(2,1)S(1)} collective-permute-done((bf16[2,128,128]{2,1,0:T(8,128)(2,1)S(1)}, bf16[2,128,128]{2,1,0:T(8,128)(2,1)S(1)}, u32[]{:S(2)}, u32[]{:S(2)}) %collective-permute-start) | collective-permute-done | bytes 65568 | tf_op jit(solution)/shard_map/while/body/eval_jaxpr/ppermute | solution.py:40
  39.0 1.2 %conditional.3 = ((f32[1,8,128]{2,1,0:T(8,128)S(1)}, f32[1,8,128]{2,1,0:T(8,128)S(1)}, f32[1,8,128,128]{3,2,1,0:T(8,128)S(1)})) conditional(s32[]{:T(128)} %convert_element_type.163, (f32[1,8,128]{2,1,0:T(8,128)S(1)}, f32[1,8,128]{2,1,0:T(8,128)S(1)}, f32[1,8,128,128]{3,2,1,0:T(8,128)S(1)}) %tuple.97, (s32[128]{0:T(128)S(1)}, s32[4]{0:T(128)S(1)}, ...), branch_computations={%region_11.11_spmd, %region_12.16_spmd} | conditional | flops 68604688 | bytes 3085976 | solution.py:175
  39.0 0.2 reduce-window.15
  39.4 0.2 fusion.62
  39.8 0.4 fusion.3
  40.3 2.3 %collective-permute-start = (bf16[2,128,128]{2,1,0:T(8,128)(2,1)S(1)}, bf16[2,128,128]{2,1,0:T(8,128)(2,1)S(1)}, u32[]{:S(2)}, u32[]{:S(2)}) collective-permute-start(bf16[2,128,128]{2,1,0:T(8,128)(2,1)S(1)} %get-tuple-element.666), channel_id=1, source_target_pairs={{0,2},{2,4},{4,6},{6,8},{8,10},{10,12},{12,14},{1,3},{3,5},{5,7},{... | collective-permute-start | bytes 196616 | tf_op jit(solution)/shard_map/while/body/eval_jaxpr/ppermute | solution.py:40
  42.6 8.1 %collective-permute-done = bf16[2,128,128]{2,1,0:T(8,128)(2,1)S(1)} collective-permute-done((bf16[2,128,128]{2,1,0:T(8,128)(2,1)S(1)}, bf16[2,128,128]{2,1,0:T(8,128)(2,1)S(1)}, u32[]{:S(2)}, u32[]{:S(2)}) %collective-permute-start) | collective-permute-done | bytes 65568 | tf_op jit(solution)/shard_map/while/body/eval_jaxpr/ppermute | solution.py:40
  50.7 1.2 %conditional.3 = ((f32[1,8,128]{2,1,0:T(8,128)S(1)}, f32[1,8,128]{2,1,0:T(8,128)S(1)}, f32[1,8,128,128]{3,2,1,0:T(8,128)S(1)})) conditional(s32[]{:T(128)} %convert_element_type.163, (f32[1,8,128]{2,1,0:T(8,128)S(1)}, f32[1,8,128]{2,1,0:T(8,128)S(1)}, f32[1,8,128,128]{3,2,1,0:T(8,128)S(1)}) %tuple.97, (s32[128]{0:T(128)S(1)}, s32[4]{0:T(128)S(1)}, ...), branch_computations={%region_11.11_spmd, %region_12.16_spmd} | conditional | flops 68604688 | bytes 3085976 | solution.py:175
  50.7 0.2 reduce-window.15
  51.1 0.2 fusion.62
  51.5 0.4 fusion.3
  52.0 1.9 %collective-permute-start = (bf16[2,128,128]{2,1,0:T(8,128)(2,1)S(1)}, bf16[2,128,128]{2,1,0:T(8,128)(2,1)S(1)}, u32[]{:S(2)}, u32[]{:S(2)}) collective-permute-start(bf16[2,128,128]{2,1,0:T(8,128)(2,1)S(1)} %get-tuple-element.666), channel_id=1, source_target_pairs={{0,2},{2,4},{4,6},{6,8},{8,10},{10,12},{12,14},{1,3},{3,5},{5,7},{... | collective-permute-start | bytes 196616 | tf_op jit(solution)/shard_map/while/body/eval_jaxpr/ppermute | solution.py:40
  53.9 5.2 %collective-permute-done = bf16[2,128,128]{2,1,0:T(8,128)(2,1)S(1)} collective-permute-done((bf16[2,128,128]{2,1,0:T(8,128)(2,1)S(1)}, bf16[2,128,128]{2,1,0:T(8,128)(2,1)S(1)}, u32[]{:S(2)}, u32[]{:S(2)}) %collective-permute-start) | collective-permute-done | bytes 65568 | tf_op jit(solution)/shard_map/while/body/eval_jaxpr/ppermute | solution.py:40
  59.1 1.2 %conditional.3 = ((f32[1,8,128]{2,1,0:T(8,128)S(1)}, f32[1,8,128]{2,1,0:T(8,128)S(1)}, f32[1,8,128,128]{3,2,1,0:T(8,128)S(1)})) conditional(s32[]{:T(128)} %convert_element_type.163, (f32[1,8,128]{2,1,0:T(8,128)S(1)}, f32[1,8,128]{2,1,0:T(8,128)S(1)}, f32[1,8,128,128]{3,2,1,0:T(8,128)S(1)}) %tuple.97, (s32[128]{0:T(128)S(1)}, s32[4]{0:T(128)S(1)}, ...), branch_computations={%region_11.11_spmd, %region_12.16_spmd} | conditional | flops 68604688 | bytes 3085976 | solution.py:175
  59.1 0.2 reduce-window.15
  59.5 0.2 fusion.62
  59.9 0.4 fusion.3
  60.4 1.9 %collective-permute-start = (bf16[2,128,128]{2,1,0:T(8,128)(2,1)S(1)}, bf16[2,128,128]{2,1,0:T(8,128)(2,1)S(1)}, u32[]{:S(2)}, u32[]{:S(2)}) collective-permute-start(bf16[2,128,128]{2,1,0:T(8,128)(2,1)S(1)} %get-tuple-element.666), channel_id=1, source_target_pairs={{0,2},{2,4},{4,6},{6,8},{8,10},{10,12},{12,14},{1,3},{3,5},{5,7},{... | collective-permute-start | bytes 196616 | tf_op jit(solution)/shard_map/while/body/eval_jaxpr/ppermute | solution.py:40
  62.4 5.1 %collective-permute-done = bf16[2,128,128]{2,1,0:T(8,128)(2,1)S(1)} collective-permute-done((bf16[2,128,128]{2,1,0:T(8,128)(2,1)S(1)}, bf16[2,128,128]{2,1,0:T(8,128)(2,1)S(1)}, u32[]{:S(2)}, u32[]{:S(2)}) %collective-permute-start) | collective-permute-done | bytes 65568 | tf_op jit(solution)/shard_map/while/body/eval_jaxpr/ppermute | solution.py:40
  67.5 1.2 %conditional.3 = ((f32[1,8,128]{2,1,0:T(8,128)S(1)}, f32[1,8,128]{2,1,0:T(8,128)S(1)}, f32[1,8,128,128]{3,2,1,0:T(8,128)S(1)})) conditional(s32[]{:T(128)} %convert_element_type.163, (f32[1,8,128]{2,1,0:T(8,128)S(1)}, f32[1,8,128]{2,1,0:T(8,128)S(1)}, f32[1,8,128,128]{3,2,1,0:T(8,128)S(1)}) %tuple.97, (s32[128]{0:T(128)S(1)}, s32[4]{0:T(128)S(1)}, ...), branch_computations={%region_11.11_spmd, %region_12.16_spmd} | conditional | flops 68604688 | bytes 3085976 | solution.py:175
  67.5 0.2 reduce-window.15
  67.9 0.2 fusion.62
  68.3 0.4 fusion.3
  68.8 1.9 %collective-permute-start = (bf16[2,128,128]{2,1,0:T(8,128)(2,1)S(1)}, bf16[2,128,128]{2,1,0:T(8,128)(2,1)S(1)}, u32[]{:S(2)}, u32[]{:S(2)}) collective-permute-start(bf16[2,128,128]{2,1,0:T(8,128)(2,1)S(1)} %get-tuple-element.666), channel_id=1, source_target_pairs={{0,2},{2,4},{4,6},{6,8},{8,10},{10,12},{12,14},{1,3},{3,5},{5,7},{... | collective-permute-start | bytes 196616 | tf_op jit(solution)/shard_map/while/body/eval_jaxpr/ppermute | solution.py:40
  70.7 5.5 %collective-permute-done = bf16[2,128,128]{2,1,0:T(8,128)(2,1)S(1)} collective-permute-done((bf16[2,128,128]{2,1,0:T(8,128)(2,1)S(1)}, bf16[2,128,128]{2,1,0:T(8,128)(2,1)S(1)}, u32[]{:S(2)}, u32[]{:S(2)}) %collective-permute-start) | collective-permute-done | bytes 65568 | tf_op jit(solution)/shard_map/while/body/eval_jaxpr/ppermute | solution.py:40
  76.3 2.4 %collective-permute-start = (bf16[2,128,128]{2,1,0:T(8,128)(2,1)S(1)}, bf16[2,128,128]{2,1,0:T(8,128)(2,1)S(1)}, u32[]{:S(2)}, u32[]{:S(2)}) collective-permute-start(bf16[2,128,128]{2,1,0:T(8,128)(2,1)S(1)} %get-tuple-element.666), channel_id=1, source_target_pairs={{0,2},{2,4},{4,6},{6,8},{8,10},{10,12},{12,14},{1,3},{3,5},{5,7},{... | collective-permute-start | bytes 196616 | tf_op jit(solution)/shard_map/while/body/eval_jaxpr/ppermute | solution.py:40
  78.6 5.4 %collective-permute-done = bf16[2,128,128]{2,1,0:T(8,128)(2,1)S(1)} collective-permute-done((bf16[2,128,128]{2,1,0:T(8,128)(2,1)S(1)}, bf16[2,128,128]{2,1,0:T(8,128)(2,1)S(1)}, u32[]{:S(2)}, u32[]{:S(2)}) %collective-permute-start) | collective-permute-done | bytes 65568 | tf_op jit(solution)/shard_map/while/body/eval_jaxpr/ppermute | solution.py:40
  84.0 1.9 %collective-permute-start = (bf16[2,128,128]{2,1,0:T(8,128)(2,1)S(1)}, bf16[2,128,128]{2,1,0:T(8,128)(2,1)S(1)}, u32[]{:S(2)}, u32[]{:S(2)}) collective-permute-start(bf16[2,128,128]{2,1,0:T(8,128)(2,1)S(1)} %get-tuple-element.666), channel_id=1, source_target_pairs={{0,2},{2,4},{4,6},{6,8},{8,10},{10,12},{12,14},{1,3},{3,5},{5,7},{... | collective-permute-start | bytes 196616 | tf_op jit(solution)/shard_map/while/body/eval_jaxpr/ppermute | solution.py:40
  86.0 5.1 %collective-permute-done = bf16[2,128,128]{2,1,0:T(8,128)(2,1)S(1)} collective-permute-done((bf16[2,128,128]{2,1,0:T(8,128)(2,1)S(1)}, bf16[2,128,128]{2,1,0:T(8,128)(2,1)S(1)}, u32[]{:S(2)}, u32[]{:S(2)}) %collective-permute-start) | collective-permute-done | bytes 65568 | tf_op jit(solution)/shard_map/while/body/eval_jaxpr/ppermute | solution.py:40
  91.1 0.2 fusion.48
  91.3 0.2 copy.87
  91.5 0.8 copy.127
  92.3 9.1 %while.37 = (s32[]{:T(128)}, f32[8,128,128]{2,1,0:T(8,128)S(1)}, s32[]{:T(128)}, bf16[8,8]{1,0:T(8,128)(2,1)S(1)}, bf16[8,8,128,128]{3,2,1,0:T(8,128)(2,1)}, /*index=5*/s32[]{:T(128)}, s32[]{:T(128)}) while((s32[]{:T(128)}, f32[8,128,128]{2,1,0:T(8,128)S(1)}, s32[]{:T(128)}, bf16[8,8]{1,0:T(8,128)(2,1)S(1)}, ...), condition=%wide.region_6.7_spmd.clone, body=%wide.region_5.6_spmd.clone.sunk | while | flops 655372 | bytes 1310913 | solution.py:34
  92.3 1.1 %fusion.73 = f32[8,128,128]{2,1,0:T(8,128)S(1)} fusion(f32[8,128,128]{2,1,0:T(8,128)S(1)} %get-tuple-element.639, bf16[8,8,128,128]{3,2,1,0:T(8,128)(2,1)} %get-tuple-element.649, s32[]{:T(128)S(6)} %copy.137, f32[8]{0:T(128)S(1)} %bitcast_convert_fusion.2, pred[]{:T(512)S(6)} %compare.4, pred[]{:T(512)S(6)} %lt.38), kind=kLoop, calls=%fused_computation.30.clone.1 | loop fusion | flops 655360 | bytes 1310758 | tf_op jit(solution)/shard_map/while/body/eval_jaxpr/jit(_where)/select_n | solution.py:32
  93.5 1.1 fusion.73
  94.6 1.1 fusion.73
  95.7 1.1 fusion.73
  96.9 1.1 fusion.73
  98.0 1.1 fusion.73
  99.1 1.1 fusion.73
  100.3 1.1 fusion.73
  101.4 0.4 convolution_bitcast_fusion.1
  101.9 0.5 multiply_reduce_fusion
  102.4 0.2 multiply_convert_fusion
  102.6 0.8 copy.88
  (98 shorter events, 2.5 us)
Async XLA Ops:
  7.2 7.0 %copy-start = (bf16[128,1024]{1,0:T(8,128)(2,1)S(1)}, bf16[128,1024]{1,0:T(8,128)(2,1)}, u32[]{:S(2)}) copy-start(bf16[128,1024]{1,0:T(8,128)(2,1)} %param.17) | copy-start | bytes 786436
  7.2 23.4 %copy-start.1 = (bf16[128,1024]{1,0:T(8,128)(2,1)S(1)}, bf16[128,1024]{1,0:T(8,128)(2,1)}, u32[]{:S(2)}) copy-start(bf16[128,1024]{1,0:T(8,128)(2,1)} %param.20) | copy-start | bytes 786436
  7.2 23.8 %copy-start.4 = (bf16[128,128]{1,0:T(8,128)(2,1)S(1)}, bf16[128,128]{1,0:T(8,128)(2,1)}, u32[]{:S(2)}) copy-start(bf16[128,128]{1,0:T(8,128)(2,1)} %param.22) | copy-start | bytes 98308
  7.2 23.8 %copy-start.3 = (bf16[128,128]{1,0:T(8,128)(2,1)S(1)}, bf16[128,128]{1,0:T(8,128)(2,1)}, u32[]{:S(2)}) copy-start(bf16[128,128]{1,0:T(8,128)(2,1)} %param.21) | copy-start | bytes 98308
  7.2 85.1 %all-gather.4.cloned.1.call-start = ((), (), s32[]{:S(2)}) async-start(), calls=%async_computation | async-start | bytes 2359296 | tf_op jit(solution)/shard_map/all_gather | solution.py:17
  15.2 16.6 %copy-start.6 = (s32[1,4]{1,0:T(1,128)S(1)}, s32[1,4]{1,0:T(1,128)}, u32[]{:S(2)}) copy-start(s32[1,4]{1,0:T(1,128)} %param.23) | copy-start | bytes 52
  31.8 7.2 %collective-permute-start = (bf16[2,128,128]{2,1,0:T(8,128)(2,1)S(1)}, bf16[2,128,128]{2,1,0:T(8,128)(2,1)S(1)}, u32[]{:S(2)}, u32[]{:S(2)}) collective-permute-start(bf16[2,128,128]{2,1,0:T(8,128)(2,1)S(1)} %get-tuple-element.666), channel_id=1, source_target_pairs={{0,2},{2,4},{4,6},{6,8},{8,10},{10,12},{12,14},{1,3},{3,5},{5,7},{... | collective-permute-start | bytes 196616 | tf_op jit(solution)/shard_map/while/body/eval_jaxpr/ppermute | solution.py:40
  40.3 10.4 %collective-permute-start = (bf16[2,128,128]{2,1,0:T(8,128)(2,1)S(1)}, bf16[2,128,128]{2,1,0:T(8,128)(2,1)S(1)}, u32[]{:S(2)}, u32[]{:S(2)}) collective-permute-start(bf16[2,128,128]{2,1,0:T(8,128)(2,1)S(1)} %get-tuple-element.666), channel_id=1, source_target_pairs={{0,2},{2,4},{4,6},{6,8},{8,10},{10,12},{12,14},{1,3},{3,5},{5,7},{... | collective-permute-start | bytes 196616 | tf_op jit(solution)/shard_map/while/body/eval_jaxpr/ppermute | solution.py:40
  52.0 7.2 %collective-permute-start = (bf16[2,128,128]{2,1,0:T(8,128)(2,1)S(1)}, bf16[2,128,128]{2,1,0:T(8,128)(2,1)S(1)}, u32[]{:S(2)}, u32[]{:S(2)}) collective-permute-start(bf16[2,128,128]{2,1,0:T(8,128)(2,1)S(1)} %get-tuple-element.666), channel_id=1, source_target_pairs={{0,2},{2,4},{4,6},{6,8},{8,10},{10,12},{12,14},{1,3},{3,5},{5,7},{... | collective-permute-start | bytes 196616 | tf_op jit(solution)/shard_map/while/body/eval_jaxpr/ppermute | solution.py:40
  60.4 7.1 %collective-permute-start = (bf16[2,128,128]{2,1,0:T(8,128)(2,1)S(1)}, bf16[2,128,128]{2,1,0:T(8,128)(2,1)S(1)}, u32[]{:S(2)}, u32[]{:S(2)}) collective-permute-start(bf16[2,128,128]{2,1,0:T(8,128)(2,1)S(1)} %get-tuple-element.666), channel_id=1, source_target_pairs={{0,2},{2,4},{4,6},{6,8},{8,10},{10,12},{12,14},{1,3},{3,5},{5,7},{... | collective-permute-start | bytes 196616 | tf_op jit(solution)/shard_map/while/body/eval_jaxpr/ppermute | solution.py:40
  68.8 7.5 %collective-permute-start = (bf16[2,128,128]{2,1,0:T(8,128)(2,1)S(1)}, bf16[2,128,128]{2,1,0:T(8,128)(2,1)S(1)}, u32[]{:S(2)}, u32[]{:S(2)}) collective-permute-start(bf16[2,128,128]{2,1,0:T(8,128)(2,1)S(1)} %get-tuple-element.666), channel_id=1, source_target_pairs={{0,2},{2,4},{4,6},{6,8},{8,10},{10,12},{12,14},{1,3},{3,5},{5,7},{... | collective-permute-start | bytes 196616 | tf_op jit(solution)/shard_map/while/body/eval_jaxpr/ppermute | solution.py:40
  76.3 7.7 %collective-permute-start = (bf16[2,128,128]{2,1,0:T(8,128)(2,1)S(1)}, bf16[2,128,128]{2,1,0:T(8,128)(2,1)S(1)}, u32[]{:S(2)}, u32[]{:S(2)}) collective-permute-start(bf16[2,128,128]{2,1,0:T(8,128)(2,1)S(1)} %get-tuple-element.666), channel_id=1, source_target_pairs={{0,2},{2,4},{4,6},{6,8},{8,10},{10,12},{12,14},{1,3},{3,5},{5,7},{... | collective-permute-start | bytes 196616 | tf_op jit(solution)/shard_map/while/body/eval_jaxpr/ppermute | solution.py:40
  84.0 7.1 %collective-permute-start = (bf16[2,128,128]{2,1,0:T(8,128)(2,1)S(1)}, bf16[2,128,128]{2,1,0:T(8,128)(2,1)S(1)}, u32[]{:S(2)}, u32[]{:S(2)}) collective-permute-start(bf16[2,128,128]{2,1,0:T(8,128)(2,1)S(1)} %get-tuple-element.666), channel_id=1, source_target_pairs={{0,2},{2,4},{4,6},{6,8},{8,10},{10,12},{12,14},{1,3},{3,5},{5,7},{... | collective-permute-start | bytes 196616 | tf_op jit(solution)/shard_map/while/body/eval_jaxpr/ppermute | solution.py:40
  92.3 9.1 %copy-start.2 = (bf16[128,1024]{1,0:T(8,128)(2,1)S(1)}, bf16[128,1024]{1,0:T(8,128)(2,1)}, u32[]{:S(2)}) copy-start(bf16[128,1024]{1,0:T(8,128)(2,1)} %param.15) | copy-start | bytes 786436
  101.4 1.0 copy-start.5
Sparse Core Ops, SparseCore 0:
  15.3 51.3 all-gather.3
where the time goes:
time: 112 us; the launch traced here: 110 us
  waiting for transfers between devices  39.1 us (35%)
  other arithmetic  15.2 us (14%)
  blocking collectives  15.1 us (13%)
  starting transfers between devices  15 us (13%)
  between operations  14.3 us (13%)
  local copies, waits for them, and re-layouts  5.7 us (5%)
  matrix products  5.15 us (5%)
    ppermute x7, waiting for transfers between devices, passed_along(): return lax.ppermute(block, axis, route)  39.1 us
    all_gather x1, blocking collectives, entering(): lax.all_gather(part.astype(kind), axis)  15.1 us
    ppermute x7, starting transfers between devices, passed_along(): return lax.ppermute(block, axis, route)  15 us
    select_n x8, other arithmetic, step(): return jax.tree.map(lambda a, b: jnp.where(reached, a, b), new, before)  8.79 us
    unnamed x20, local copies, waits for them, and re-layouts  2.79 us
  transfers between devices with their start and end apart: 8, of which 7 were waited for; matrix products, arithmetic and copies ran while one was open for 7% of the time, Pallas kernels for 0%

commit v1 on v0

--- a/solution.py
+++ b/solution.py
@@ -1,8 +1,11 @@
+import functools
 import math
 
 import jax
 import jax.numpy as jnp
 from jax import lax
+from jax.experimental import pallas as pl
+from jax.experimental.pallas import tpu as pltpu
 from jax.sharding import PartitionSpec as P
 
 HEAD_DIM = 128
@@ -185,6 +188,329 @@
     return (lin_out, soft_out)
 
 
+def block_kernel(
+    span,
+    heads,
+    lens,
+    lin_q,
+    lin_k,
+    lin_v,
+    forget,
+    gain,
+    soft_q,
+    soft_k,
+    soft_v,
+    lin_out,
+    soft_out,
+    keys,
+    values,
+    bias,
+    local,
+    packed,
+    paired,
+    carries,
+    carries_in,
+    arrived,
+    onward,
+    across,
+    incoming,
+    intra,
+    queried,
+    send_kv,
+    recv_kv,
+    send_pair,
+    recv_pair,
+    send_carry,
+    recv_carry,
+    send_chain,
+    recv_chain,
+    send_state,
+    recv_state,
+):
+    f32, bf16 = jnp.float32, jnp.bfloat16
+    rows = lin_q.shape[0]
+    width = HEAD_DIM
+    half = heads // 2
+    window = span // 2
+    me = lax.axis_index("seq")
+    z, x = me // 2, me % 2
+    other = me + 1 - 2 * x
+    mesh_id = pl.DeviceIdType.MESH
+
+    barrier = pltpu.get_barrier_semaphore()
+    for d in range(1, window + 1):
+        for target, ok in ((me + d, me + d < span), (me - d, me >= d)):
+
+            @pl.when(ok)
+            def _():
+                pl.semaphore_signal(
+                    barrier, inc=1, device_id={"seq": target}, device_id_type=mesh_id
+                )
+
+    def remote(src, dst, send, recv, target):
+        return pltpu.make_async_remote_copy(
+            src_ref=src,
+            dst_ref=dst,
+            send_sem=send,
+            recv_sem=recv,
+            device_id={"seq": target},
+            device_id_type=mesh_id,
+        )
+
+    def kv_copy(d, which):
+        src, dst = ((soft_k, keys), (soft_v, values))[which]
+        return remote(
+            src,
+            dst.at[pl.ds(d * rows, rows)],
+            send_kv.at[2 * d - 2 + which],
+            recv_kv.at[2 * d - 2 + which],
+            me + d,
+        )
+
+    def pair_copy(i):
+        return remote(
+            packed.at[half * (1 - x) + i], paired.at[i], send_pair.at[i], recv_pair.at[i], other
+        )
+
+    def carry_copy():
+        return remote(carries, carries_in, send_carry, recv_carry, other)
+
+    def chain_copy(i):
+        return remote(onward.at[i], arrived.at[i], send_chain.at[i], recv_chain.at[i], me + 2)
+
+    def state_copy(i):
+        return remote(
+            across.at[i], incoming.at[half * x + i], send_state.at[i], recv_state.at[i], other
+        )
+
+    first = me * rows
+    starts = [jnp.int32(0)]
+    for i in range(lens.shape[1] - 1):
+        starts.append(starts[-1] + lens[0, i])
+    where_col = first + lax.broadcasted_iota(jnp.int32, (rows, 1), 0)
+    doc_col = jnp.zeros((rows, 1), jnp.int32)
+    live_col = jnp.ones((rows, 1), f32)
+    last = first + rows - 1
+    doc_last = jnp.int32(0)
+    live_last = jnp.float32(1.0)
+    for s in starts:
+        doc_col = jnp.maximum(doc_col, jnp.where(where_col >= s, s, 0))
+        live_col = jnp.where((where_col >= s) & (s >= first), 0.0, live_col)
+        doc_last = jnp.maximum(doc_last, jnp.where(last >= s, s, 0))
+        live_last = jnp.where((last >= s) & (s >= first), 0.0, live_last)
+
+    t_at = lax.broadcasted_iota(jnp.int32, (rows, rows), 0)
+    s_at = lax.broadcasted_iota(jnp.int32, (rows, rows), 1)
+    tri = (s_at <= t_at).astype(f32)
+    logs = forget[...]
+    cum = lax.dot_general(
+        tri, logs, (((1,), (0,)), ((), ())), precision=lax.Precision.HIGHEST,
+        preferred_element_type=f32,
+    )
+    cum_rows = lax.dot_general(
+        logs, tri, (((0,), (1,)), ((), ())), precision=lax.Precision.HIGHEST,
+        preferred_element_type=f32,
+    )
+    end = cum[rows - 1 : rows, :]
+    tail_mask = where_col >= doc_last
+    tail = jnp.where(tail_mask, jnp.exp(jnp.where(tail_mask, end - cum, 0.0)), 0.0)
+    entry = jnp.exp(cum) * live_col
+    carries[...] = jnp.broadcast_to(jnp.exp(cum_rows[:, rows - 1 : rows]) * live_last, carries.shape)
+
+    def head(ref, h):
+        return ref[:, h * width : (h + 1) * width]
+
+    for h in range(heads):
+        keyed = (head(lin_k, h).astype(f32) * tail[:, h : h + 1]).astype(bf16)
+        state = lax.dot_general(
+            keyed, head(lin_v, h), (((0,), (0,)), ((), ())), preferred_element_type=f32
+        )
+        local[h] = state
+        packed[h] = state.astype(bf16)
+
+    peers = jnp.minimum(me, window) + jnp.minimum(span - 1 - me, window)
+    pl.semaphore_wait(barrier, peers)
+
+    carry_copy().start()
+    for i in range(half):
+        pair_copy(i).start()
+    for d in range(1, window + 1):
+
+        @pl.when(me + d < span)
+        def _():
+            kv_copy(d, 0).start()
+            kv_copy(d, 1).start()
+
+        @pl.when(me < d)
+        def _():
+            keys[d * rows : (d + 1) * rows, :] = jnp.zeros((rows, width), bf16)
+            values[d * rows : (d + 1) * rows, :] = jnp.zeros((rows, width), bf16)
+
+    keys[0:rows, :] = soft_k[...]
+    values[0:rows, :] = soft_v[...]
+
+    mask = (s_at <= t_at) & (first + s_at >= doc_col)
+    bias[:, 0:rows] = jnp.where(mask, 0.0, NEGATIVE)
+    for d in range(1, window + 1):
+        bias[:, d * rows : (d + 1) * rows] = jnp.where(
+            first - d * rows + s_at >= doc_col, 0.0, NEGATIVE
+        )
+    for h in range(heads):
+        query = head(lin_q, h)
+        diff = cum[:, h : h + 1] - cum_rows[h : h + 1, :]
+        decay = jnp.where(mask, jnp.exp(jnp.where(mask, diff, 0.0)), 0.0)
+        scores = lax.dot_general(
+            query, head(lin_k, h), (((1,), (1,)), ((), ())), preferred_element_type=f32
+        )
+        intra[h] = jnp.dot(
+            (scores * decay).astype(bf16), head(lin_v, h), preferred_element_type=f32
+        )
+        queried[h] = (query.astype(f32) * entry[:, h : h + 1]).astype(bf16)
+
+    carry_copy().wait_recv()
+    even = x == 0
+    for i in range(half):
+        h = half * x + i
+        pair_copy(i).wait_recv()
+        own, far = local[h], paired[i].astype(f32)
+        own_carry, far_carry = carries[pl.ds(h, 1), :], carries_in[pl.ds(h, 1), :]
+        early, late = jnp.where(even, own, far), jnp.where(even, far, own)
+        early_carry = jnp.where(even, own_carry, far_carry)
+        late_carry = jnp.where(even, far_carry, own_carry)
+
+        @pl.when(z == 0)
+        def _():
+            arrived[i] = jnp.zeros((width, width), bf16)
+
+        @pl.when(z > 0)
+        def _():
+            chain_copy(i).wait_recv()
+
+        entering_even = arrived[i].astype(f32)
+        entering_odd = early + early_carry * entering_even
+        onward[i] = (late + late_carry * entering_odd).astype(bf16)
+
+        @pl.when(me + 2 < span)
+        def _():
+            chain_copy(i).start()
+
+        incoming[h] = jnp.where(even, entering_even, entering_odd).astype(bf16)
+        across[i] = jnp.where(even, entering_odd, entering_even).astype(bf16)
+        state_copy(i).start()
+
+    for d in range(1, window + 1):
+
+        @pl.when(me >= d)
+        def _():
+            kv_copy(d, 0).wait_recv()
+            kv_copy(d, 1).wait_recv()
+
+    factor = math.log2(math.e) / math.sqrt(width)
+    for h in range(heads):
+        scores = lax.dot_general(
+            head(soft_q, h), keys[...], (((1,), (1,)), ((), ())), preferred_element_type=f32
+        )
+        scores = scores + bias[...]
+        peak = jnp.max(scores, axis=1, keepdims=True)
+        weights = jnp.exp2((scores - peak) * factor)
+        total = jnp.sum(weights, axis=1, keepdims=True)
+        numer = jnp.dot(weights.astype(bf16), values[...], preferred_element_type=f32)
+        soft_out[:, h * width : (h + 1) * width] = (numer / total).astype(bf16)
+
+    for i in range(half):
+        state_copy(i).wait_recv()
+    for h in range(heads):
+        summed = intra[h] + jnp.dot(queried[h], incoming[h], preferred_element_type=f32)
+        mean_square = jnp.mean(summed * summed, axis=1, keepdims=True)
+        normed = summed * lax.rsqrt(mean_square + 1e-06) * head(gain, h)
+        lin_out[:, h * width : (h + 1) * width] = normed.astype(bf16)
+
+    carry_copy().wait_send()
+    for i in range(half):
+        pair_copy(i).wait_send()
+        state_copy(i).wait_send()
+
+        @pl.when(me + 2 < span)
+        def _():
+            chain_copy(i).wait_send()
+
+    for d in range(1, window + 1):
+
+        @pl.when(me + d < span)
+        def _():
+            kv_copy(d, 0).wait_send()
+            kv_copy(d, 1).wait_send()
+
+
+def in_one_kernel(
+    lin_query,
+    lin_key,
+    lin_value,
+    forget_log,
+    norm_gain,
+    soft_query,
+    soft_key,
+    soft_value,
+    doc_lengths,
+):
+    span = lax.axis_size("seq")
+    rows, columns = lin_query.shape
+    heads = columns // HEAD_DIM
+    half, window = heads // 2, span // 2
+    f32, bf16 = jnp.float32, jnp.bfloat16
+    dma = pltpu.SemaphoreType.DMA
+    whole = pl.BlockSpec(memory_space=pltpu.VMEM)
+    square = (HEAD_DIM, HEAD_DIM)
+    return pl.pallas_call(
+        functools.partial(block_kernel, span, heads),
+        out_shape=(
+            jax.ShapeDtypeStruct((rows, columns), bf16),
+            jax.ShapeDtypeStruct((rows, columns), bf16),
+        ),
+        in_specs=[pl.BlockSpec(memory_space=pltpu.SMEM)] + [whole] * 8,
+        out_specs=(whole, whole),
+        scratch_shapes=[
+            pltpu.VMEM(((window + 1) * rows, HEAD_DIM), bf16),
+            pltpu.VMEM(((window + 1) * rows, HEAD_DIM), bf16),
+            pltpu.VMEM((rows, (window + 1) * rows), f32),
+            pltpu.VMEM((heads, *square), f32),
+            pltpu.VMEM((heads, *square), bf16),
+            pltpu.VMEM((half, *square), bf16),
+            pltpu.VMEM((heads, HEAD_DIM), f32),
+            pltpu.VMEM((heads, HEAD_DIM), f32),
+            pltpu.VMEM((half, *square), bf16),
+            pltpu.VMEM((half, *square), bf16),
+            pltpu.VMEM((half, *square), bf16),
+            pltpu.VMEM((heads, *square), bf16),
+            pltpu.VMEM((heads, rows, HEAD_DIM), f32),
+            pltpu.VMEM((heads, rows, HEAD_DIM), bf16),
+            dma((2 * window,)),
+            dma((2 * window,)),
+            dma((half,)),
+            dma((half,)),
+            dma,
+            dma,
+            dma((half,)),
+            dma((half,)),
+            dma((half,)),
+            dma((half,)),
+        ],
+        compiler_params=pltpu.CompilerParams(
+            collective_id=0, has_side_effects=True, vmem_limit_bytes=32 << 20
+        ),
+    )(
+        doc_lengths,
+        lin_query,
+        lin_key,
+        lin_value,
+        forget_log,
+        norm_gain.reshape(1, columns),
+        soft_query,
+        soft_key,
+        soft_value,
+    )
+
+
 def solution(mesh):
     placed = (
         P(("rep", "seq"), "sub"),
@@ -197,8 +523,9 @@
         P(("rep", "seq"), "sub"),
         P("rep", None),
     )
+    small = mesh.shape["seq"] == 8
     return jax.shard_map(
-        per_device,
+        in_one_kernel if small else per_device,
         mesh=mesh,
         in_specs=placed,
         out_specs=(P(("rep", "seq"), "sub"), P(("rep", "seq"), "sub")),

time: 112 us -> 28.9 us (0.26)
  the two profiles are of different devices: /device:TPU:20 before, /device:TPU:24 now
where the time goes in v1:
time: 28.9 us; the launch traced here: 28.6 us
  Pallas kernels  21.8 us (75%)
  local copies, waits for them, and re-layouts  6.03 us (21%)
  between operations  0.71 us (2%)
    pallas_call x1, Pallas kernels, in_one_kernel(): pl.pallas_call(functools.partial(block_kernel, span, heads), out_shape=(j...  21.8 us
    unnamed x19, local copies, waits for them, and re-layouts  6.03 us

profile of v1, /device:TPU:24, one launch (start us, length us, event | category | flops | bytes accessed | tf_op | source)
XLA Modules:
  0.0 28.6 jit_solution(10106682773842993794)
XLA Ops:
  0.6 0.0 copy-start.7
  0.6 0.0 copy-start.4
  0.7 0.0 copy-start.5
  0.7 0.0 copy-start.6
  0.7 0.8 %copy.11.forget = f32[128,8]{1,0:T(8,128)S(1)} copy(f32[128,8]{0,1:T(8,128)} %param.12) | data formatting | bytes 8192 | tf_op args[3]
  1.5 0.0 copy-done.7
  1.5 0.0 copy-done.4
  1.5 0.0 copy-done.5
  1.5 0.0 copy-done.6
  1.5 0.0 copy-start
  1.5 0.9 %copy-done = bf16[128,1024]{1,0:T(8,128)(2,1)S(1)} copy-done((bf16[128,1024]{1,0:T(8,128)(2,1)S(1)}, bf16[128,1024]{1,0:T(8,128)(2,1)}, u32[]{:S(2)}) %copy-start) | copy-done | bytes 262168
  2.5 0.0 copy-start.1
  2.5 0.9 %copy-done.1 = bf16[128,1024]{1,0:T(8,128)(2,1)S(1)} copy-done((bf16[128,1024]{1,0:T(8,128)(2,1)S(1)}, bf16[128,1024]{1,0:T(8,128)(2,1)}, u32[]{:S(2)}) %copy-start.1) | copy-done | bytes 262168
  3.4 0.0 copy-start.2
  3.4 0.9 %copy-done.2 = bf16[128,1024]{1,0:T(8,128)(2,1)S(1)} copy-done((bf16[128,1024]{1,0:T(8,128)(2,1)S(1)}, bf16[128,1024]{1,0:T(8,128)(2,1)}, u32[]{:S(2)}) %copy-start.2) | copy-done | bytes 262168
  4.4 0.0 copy-start.3
  4.4 0.9 %copy-done.3 = bf16[128,1024]{1,0:T(8,128)(2,1)S(1)} copy-done((bf16[128,1024]{1,0:T(8,128)(2,1)S(1)}, bf16[128,1024]{1,0:T(8,128)(2,1)}, u32[]{:S(2)}) %copy-start.3) | copy-done | bytes 262168
  5.3 21.8 %shard_map.104 = (bf16[128,1024]{1,0:T(8,128)(2,1)S(1)}, bf16[128,1024]{1,0:T(8,128)(2,1)S(1)}) custom-call(s32[1,4]{1,0:T(1,128)S(1)} %copy-done.7, bf16[128,1024]{1,0:T(8,128)(2,1)S(1)} %copy-done, bf16[128,1024]{1,0:T(8,128)(2,1)S(1)} %copy-done.1, bf16[128,1024]{1,0:T(8,128)(2,1)S(1)} %copy-done.2, f32[128,8]{1,0:T(8,128)S(1)} %copy.11.forget, ...), custom_call_target="tpu_custom_call" | custom-call | tf_op jit(solution)/shard_map/pallas_call | solution.py:464
  27.2 0.7 %copy.14 = bf16[128,1024]{1,0:T(8,128)(2,1)} copy(bf16[128,1024]{1,0:T(8,128)(2,1)S(1)} %get-tuple-element.4) | data formatting | bytes 524288
  27.9 0.7 %copy.15 = bf16[128,1024]{1,0:T(8,128)(2,1)} copy(bf16[128,1024]{1,0:T(8,128)(2,1)S(1)} %get-tuple-element.5) | data formatting | bytes 524288
Async XLA Ops:
  0.6 0.9 %copy-start.7 = (s32[1,4]{1,0:T(1,128)S(1)}, s32[1,4]{1,0:T(1,128)}, u32[]{:S(2)}) copy-start(s32[1,4]{1,0:T(1,128)} %lens.1) | copy-start | bytes 52
  0.6 0.8 %copy-start.4 = (bf16[128,128]{1,0:T(8,128)(2,1)S(1)}, bf16[128,128]{1,0:T(8,128)(2,1)}, u32[]{:S(2)}) copy-start(bf16[128,128]{1,0:T(8,128)(2,1)} %soft_k.1) | copy-start | bytes 98308
  0.7 0.8 %copy-start.5 = (bf16[128,128]{1,0:T(8,128)(2,1)S(1)}, bf16[128,128]{1,0:T(8,128)(2,1)}, u32[]{:S(2)}) copy-start(bf16[128,128]{1,0:T(8,128)(2,1)} %soft_v.1) | copy-start | bytes 98308
  0.7 0.8 %copy-start.6 = (f32[1024]{0:T(1024)S(1)}, f32[1024]{0:T(1024)}, u32[]{:S(2)}) copy-start(f32[1024]{0:T(1024)} %param.13) | copy-start | bytes 12292
  1.5 1.0 %copy-start = (bf16[128,1024]{1,0:T(8,128)(2,1)S(1)}, bf16[128,1024]{1,0:T(8,128)(2,1)}, u32[]{:S(2)}) copy-start(bf16[128,1024]{1,0:T(8,128)(2,1)} %lin_q.1) | copy-start | bytes 786436
  2.5 0.9 %copy-start.1 = (bf16[128,1024]{1,0:T(8,128)(2,1)S(1)}, bf16[128,1024]{1,0:T(8,128)(2,1)}, u32[]{:S(2)}) copy-start(bf16[128,1024]{1,0:T(8,128)(2,1)} %lin_k.1) | copy-start | bytes 786436
  3.4 0.9 %copy-start.2 = (bf16[128,1024]{1,0:T(8,128)(2,1)S(1)}, bf16[128,1024]{1,0:T(8,128)(2,1)}, u32[]{:S(2)}) copy-start(bf16[128,1024]{1,0:T(8,128)(2,1)} %lin_v.1) | copy-start | bytes 786436
  4.4 0.9 %copy-start.3 = (bf16[128,1024]{1,0:T(8,128)(2,1)S(1)}, bf16[128,1024]{1,0:T(8,128)(2,1)}, u32[]{:S(2)}) copy-start(bf16[128,1024]{1,0:T(8,128)(2,1)} %soft_q.1) | copy-start | bytes 786436

commit v2 on v1

--- a/solution.py
+++ b/solution.py
@@ -192,18 +192,23 @@
     span,
     heads,
     lens,
+    lin_q_far,
+    lin_k_far,
+    lin_v_far,
+    forget_far,
+    gain_far,
+    soft_q_far,
+    soft_k_far,
+    soft_v_far,
+    lin_out,
+    soft_out,
     lin_q,
     lin_k,
     lin_v,
     forget,
     gain,
     soft_q,
-    soft_k,
-    soft_v,
-    lin_out,
-    soft_out,
-    keys,
-    values,
+    pairs,
     bias,
     local,
     packed,
@@ -216,6 +221,7 @@
     incoming,
     intra,
     queried,
+    loads,
     send_kv,
     recv_kv,
     send_pair,
@@ -237,15 +243,33 @@
     other = me + 1 - 2 * x
     mesh_id = pl.DeviceIdType.MESH
 
+    def load(i):
+        src, dst = (
+            (soft_k_far, pairs.at[0, 0]),
+            (soft_v_far, pairs.at[0, 1]),
+            (forget_far, forget),
+            (lin_k_far, lin_k),
+            (lin_v_far, lin_v),
+            (lin_q_far, lin_q),
+            (soft_q_far, soft_q),
+            (gain_far, gain),
+        )[i]
+        return pltpu.make_async_copy(src, dst, loads.at[i])
+
     barrier = pltpu.get_barrier_semaphore()
-    for d in range(1, window + 1):
-        for target, ok in ((me + d, me + d < span), (me - d, me >= d)):
-
-            @pl.when(ok)
-            def _():
-                pl.semaphore_signal(
-                    barrier, inc=1, device_id={"seq": target}, device_id_type=mesh_id
-                )
+    near = [(other, True)]
+    for d in (2, 4):
+        near += [(me + d, me + d < span), (me - d, me >= d)]
+    peers = 0
+    for target, ok in near:
+        peers = peers + jnp.int32(ok)
+
+        @pl.when(ok)
+        def _():
+            pl.semaphore_signal(barrier, inc=1, device_id={"seq": target}, device_id_type=mesh_id)
+
+    for i in range(8):
+        load(i).start()
 
     def remote(src, dst, send, recv, target):
         return pltpu.make_async_remote_copy(
@@ -257,15 +281,20 @@
             device_id_type=mesh_id,
         )
 
-    def kv_copy(d, which):
-        src, dst = ((soft_k, keys), (soft_v, values))[which]
-        return remote(
-            src,
-            dst.at[pl.ds(d * rows, rows)],
-            send_kv.at[2 * d - 2 + which],
-            recv_kv.at[2 * d - 2 + which],
-            me + d,
-        )
+    def kv_copy(held, slot, ahead):
+        return remote(pairs.at[held], pairs.at[slot], send_kv.at[slot], recv_kv.at[slot], me + ahead)
+
+    first_column, second_column = x == 0, x == 1
+    kv_sent = (
+        (0, 2, 2, me + 2 < span),
+        (0, 4, 4, me + 4 < span),
+        (0, 1, 1, first_column),
+    )
+    kv_passed = (
+        (2, 3, 1, first_column & (me >= 2)),
+        (2, 1, -1, second_column & (me >= 2)),
+        (4, 3, -1, second_column & (me >= 4)),
+    )
 
     def pair_copy(i):
         return remote(
@@ -282,6 +311,15 @@
         return remote(
             across.at[i], incoming.at[half * x + i], send_state.at[i], recv_state.at[i], other
         )
+
+    load(0).wait()
+    load(1).wait()
+    pl.semaphore_wait(barrier, peers)
+    for held, slot, ahead, ok in kv_sent:
+
+        @pl.when(ok)
+        def _():
+            kv_copy(held, slot, ahead).start()
 
     first = me * rows
     starts = [jnp.int32(0)]
@@ -302,13 +340,14 @@
     t_at = lax.broadcasted_iota(jnp.int32, (rows, rows), 0)
     s_at = lax.broadcasted_iota(jnp.int32, (rows, rows), 1)
     tri = (s_at <= t_at).astype(f32)
+    load(2).wait()
     logs = forget[...]
     cum = lax.dot_general(
-        tri, logs, (((1,), (0,)), ((), ())), precision=lax.Precision.HIGHEST,
+        tri, logs, (((1,), (1,)), ((), ())), precision=lax.Precision.HIGHEST,
         preferred_element_type=f32,
     )
     cum_rows = lax.dot_general(
-        logs, tri, (((0,), (1,)), ((), ())), precision=lax.Precision.HIGHEST,
+        logs, tri, (((1,), (1,)), ((), ())), precision=lax.Precision.HIGHEST,
         preferred_element_type=f32,
     )
     end = cum[rows - 1 : rows, :]
@@ -320,6 +359,8 @@
     def head(ref, h):
         return ref[:, h * width : (h + 1) * width]
 
+    load(3).wait()
+    load(4).wait()
     for h in range(heads):
         keyed = (head(lin_k, h).astype(f32) * tail[:, h : h + 1]).astype(bf16)
         state = lax.dot_general(
@@ -328,26 +369,14 @@
         local[h] = state
         packed[h] = state.astype(bf16)
 
-    peers = jnp.minimum(me, window) + jnp.minimum(span - 1 - me, window)
-    pl.semaphore_wait(barrier, peers)
-
     carry_copy().start()
     for i in range(half):
         pair_copy(i).start()
     for d in range(1, window + 1):
 
-        @pl.when(me + d < span)
-        def _():
-            kv_copy(d, 0).start()
-            kv_copy(d, 1).start()
-
         @pl.when(me < d)
         def _():
-            keys[d * rows : (d + 1) * rows, :] = jnp.zeros((rows, width), bf16)
-            values[d * rows : (d + 1) * rows, :] = jnp.zeros((rows, width), bf16)
-
-    keys[0:rows, :] = soft_k[...]
-    values[0:rows, :] = soft_v[...]
+            pairs[d] = jnp.zeros((2, rows, width), bf16)
 
     mask = (s_at <= t_at) & (first + s_at >= doc_col)
     bias[:, 0:rows] = jnp.where(mask, 0.0, NEGATIVE)
@@ -355,6 +384,7 @@
         bias[:, d * rows : (d + 1) * rows] = jnp.where(
             first - d * rows + s_at >= doc_col, 0.0, NEGATIVE
         )
+    load(5).wait()
     for h in range(heads):
         query = head(lin_q, h)
         diff = cum[:, h : h + 1] - cum_rows[h : h + 1, :]
@@ -366,6 +396,50 @@
             (scores * decay).astype(bf16), head(lin_v, h), preferred_element_type=f32
         )
         queried[h] = (query.astype(f32) * entry[:, h : h + 1]).astype(bf16)
+
+    for d in (2, 4):
+
+        @pl.when(me >= d)
+        def _():
+            kv_copy(0, d, d).wait_recv()
+
+    for held, slot, ahead, ok in kv_passed:
+
+        @pl.when(ok)
+        def _():
+            kv_copy(held, slot, ahead).start()
+
+    load(6).wait()
+    load(7).wait()
+
+    def softmax():
+        key_rows = pairs[:, 0].reshape((window + 1) * rows, width)
+        value_rows = pairs[:, 1].reshape((window + 1) * rows, width)
+        factor = math.log2(math.e) / math.sqrt(width)
+        for h in range(heads):
+            scores = lax.dot_general(
+                head(soft_q, h), key_rows, (((1,), (1,)), ((), ())), preferred_element_type=f32
+            )
+            scores = scores + bias[...]
+            peak = jnp.max(scores, axis=1, keepdims=True)
+            weights = jnp.exp2((scores - peak) * factor)
+            total = jnp.sum(weights, axis=1, keepdims=True)
+            numer = jnp.dot(weights.astype(bf16), value_rows, preferred_element_type=f32)
+            soft_out[:, h * width : (h + 1) * width] = (numer / total).astype(bf16)
+
+    def odd_slots():
+        for d in (1, 3):
+
+            @pl.when(me >= d)
+            def _():
+                kv_copy(0, d, 1).wait_recv()
+
+    z_last = span // 2 - 1
+
+    @pl.when(z == z_last)
+    def _():
+        odd_slots()
+        softmax()
 
     carry_copy().wait_recv()
     even = x == 0
@@ -398,24 +472,10 @@
         across[i] = jnp.where(even, entering_odd, entering_even).astype(bf16)
         state_copy(i).start()
 
-    for d in range(1, window + 1):
-
-        @pl.when(me >= d)
-        def _():
-            kv_copy(d, 0).wait_recv()
-            kv_copy(d, 1).wait_recv()
-
-    factor = math.log2(math.e) / math.sqrt(width)
-    for h in range(heads):
-        scores = lax.dot_general(
-            head(soft_q, h), keys[...], (((1,), (1,)), ((), ())), preferred_element_type=f32
-        )
-        scores = scores + bias[...]
-        peak = jnp.max(scores, axis=1, keepdims=True)
-        weights = jnp.exp2((scores - peak) * factor)
-        total = jnp.sum(weights, axis=1, keepdims=True)
-        numer = jnp.dot(weights.astype(bf16), values[...], preferred_element_type=f32)
-        soft_out[:, h * width : (h + 1) * width] = (numer / total).astype(bf16)
+    @pl.when(z < z_last)
+    def _():
+        odd_slots()
+        softmax()
 
     for i in range(half):
         state_copy(i).wait_recv()
@@ -434,12 +494,11 @@
         def _():
             chain_copy(i).wait_send()
 
-    for d in range(1, window + 1):
-
-        @pl.when(me + d < span)
-        def _():
-            kv_copy(d, 0).wait_send()
-            kv_copy(d, 1).wait_send()
+    for held, slot, ahead, ok in kv_sent + kv_passed:
+
+        @pl.when(ok)
+        def _():
+            kv_copy(held, slot, ahead).wait_send()
 
 
 def in_one_kernel(
@@ -467,11 +526,17 @@
             jax.ShapeDtypeStruct((rows, columns), bf16),
             jax.ShapeDtypeStruct((rows, columns), bf16),
         ),
-        in_specs=[pl.BlockSpec(memory_space=pltpu.SMEM)] + [whole] * 8,
+        in_specs=[pl.BlockSpec(memory_space=pltpu.SMEM)]
+        + [pl.BlockSpec(memory_space=pltpu.HBM)] * 8,
         out_specs=(whole, whole),
         scratch_shapes=[
-            pltpu.VMEM(((window + 1) * rows, HEAD_DIM), bf16),
-            pltpu.VMEM(((window + 1) * rows, HEAD_DIM), bf16),
+            pltpu.VMEM((rows, columns), bf16),
+            pltpu.VMEM((rows, columns), bf16),
+            pltpu.VMEM((rows, columns), bf16),
+            pltpu.VMEM((heads, rows), f32),
+            pltpu.VMEM((1, columns), f32),
+            pltpu.VMEM((rows, columns), bf16),
+            pltpu.VMEM((window + 1, 2, rows, HEAD_DIM), bf16),
             pltpu.VMEM((rows, (window + 1) * rows), f32),
             pltpu.VMEM((heads, *square), f32),
             pltpu.VMEM((heads, *square), bf16),
@@ -484,8 +549,9 @@
             pltpu.VMEM((heads, *square), bf16),
             pltpu.VMEM((heads, rows, HEAD_DIM), f32),
             pltpu.VMEM((heads, rows, HEAD_DIM), bf16),
-            dma((2 * window,)),
-            dma((2 * window,)),
+            dma((8,)),
+            dma((window + 1,)),
+            dma((window + 1,)),
             dma((half,)),
             dma((half,)),
             dma,
@@ -496,14 +562,14 @@
             dma((half,)),
         ],
         compiler_params=pltpu.CompilerParams(
-            collective_id=0, has_side_effects=True, vmem_limit_bytes=32 << 20
+            collective_id=0, has_side_effects=True, vmem_limit_bytes=62 << 20
         ),
     )(
         doc_lengths,
         lin_query,
         lin_key,
         lin_value,
-        forget_log,
+        forget_log.T,
         norm_gain.reshape(1, columns),
         soft_query,
         soft_key,

time: 28.9 us -> 25 us (0.87)
  local copies, waits for them, and re-layouts: 6.03 us -> 2.42 us
    unnamed x19 -> x4, local copies, waits for them, and re-layouts: 6.03 us -> 2.42 us
where the time goes in v2:
time: 25 us; the launch traced here: 24.8 us
  Pallas kernels  21.8 us (87%)
  local copies, waits for them, and re-layouts  2.42 us (10%)
  between operations  0.65 us (3%)
    pallas_call x1, Pallas kernels, in_one_kernel(): pl.pallas_call(functools.partial(block_kernel, span, heads), out_shape=(j...  21.8 us
    unnamed x4, local copies, waits for them, and re-layouts  2.42 us

profile of v2, /device:TPU:24, one launch (start us, length us, event | category | flops | bytes accessed | tf_op | source)
XLA Modules:
  0.0 24.8 jit_solution(16995217490609854917)
XLA Ops:
  0.6 21.8 %shard_map.104 = (bf16[128,1024]{1,0:T(8,128)(2,1)}, bf16[128,1024]{1,0:T(8,128)(2,1)}) custom-call(s32[1,4]{1,0:T(1,128)} %lens.1, bf16[128,1024]{1,0:T(8,128)(2,1)} %lin_q_far.1, bf16[128,1024]{1,0:T(8,128)(2,1)} %lin_k_far.1, bf16[128,1024]{1,0:T(8,128)(2,1)} %lin_v_far.1, f32[8,128]{1,0:T(8,128)} %bitcast.2, f32[1,1024]{1,0:T(1,128)} %bitcast.3, ...), custom_call_target="tpu_custom_call" | custom-call | tf_op jit(solution)/shard_map/pallas_call | solution.py:523
  22.4 0.0 copy-start
  22.4 1.7 %copy.13 = bf16[128,1024]{1,0:T(8,128)(2,1)} copy(bf16[128,1024]{1,0:T(8,128)(2,1)} %get-tuple-element.4) | data formatting | bytes 524288
  24.1 0.0 copy-done
  24.1 0.7 %copy.14 = bf16[128,1024]{1,0:T(8,128)(2,1)} copy(bf16[128,1024]{1,0:T(8,128)(2,1)S(1)} %copy-done) | data formatting | bytes 524288
Async XLA Ops:
  22.4 1.7 %copy-start = (bf16[128,1024]{1,0:T(8,128)(2,1)S(1)}, bf16[128,1024]{1,0:T(8,128)(2,1)}, u32[]{:S(2)}) copy-start(bf16[128,1024]{1,0:T(8,128)(2,1)} %get-tuple-element.5) | copy-start | bytes 786436

commit v3 on v2

--- a/solution.py
+++ b/solution.py
@@ -217,11 +217,16 @@
     carries_in,
     arrived,
     onward,
+    early_in,
+    ahead_of,
     across,
     incoming,
     intra,
     queried,
+    lin_part,
+    soft_part,
     loads,
+    stores,
     send_kv,
     recv_kv,
     send_pair,
@@ -230,6 +235,8 @@
     recv_carry,
     send_chain,
     recv_chain,
+    send_early,
+    recv_early,
     send_state,
     recv_state,
 ):
@@ -288,8 +295,8 @@
     kv_sent = (
         (0, 2, 2, me + 2 < span),
         (0, 4, 4, me + 4 < span),
-        (0, 1, 1, first_column),
-    )
+    )
+    kv_beside = ((0, 1, 1, first_column),)
     kv_passed = (
         (2, 3, 1, first_column & (me >= 2)),
         (2, 1, -1, second_column & (me >= 2)),
@@ -298,7 +305,7 @@
 
     def pair_copy(i):
         return remote(
-            packed.at[half * (1 - x) + i], paired.at[i], send_pair.at[i], recv_pair.at[i], other
+            packed.at[i], paired.at[i], send_pair.at[i], recv_pair.at[i], other
         )
 
     def carry_copy():
@@ -306,6 +313,9 @@
 
     def chain_copy(i):
         return remote(onward.at[i], arrived.at[i], send_chain.at[i], recv_chain.at[i], me + 2)
+
+    def early_copy(i):
+        return remote(ahead_of.at[i], early_in.at[i], send_early.at[i], recv_early.at[i], me + 2)
 
     def state_copy(i):
         return remote(
@@ -359,19 +369,34 @@
     def head(ref, h):
         return ref[:, h * width : (h + 1) * width]
 
+    even = x == 0
+
+    def lanes(h):
+        return pl.ds(pl.multiple_of(h * width, width), width)
+
+    carry_copy().start()
     load(3).wait()
     load(4).wait()
-    for h in range(heads):
-        keyed = (head(lin_k, h).astype(f32) * tail[:, h : h + 1]).astype(bf16)
-        state = lax.dot_general(
-            keyed, head(lin_v, h), (((0,), (0,)), ((), ())), preferred_element_type=f32
-        )
-        local[h] = state
-        packed[h] = state.astype(bf16)
-
-    carry_copy().start()
-    for i in range(half):
-        pair_copy(i).start()
+    for mine in (False, True):
+        for i in range(half):
+            h = half * x + i if mine else half * (1 - x) + i
+            low, high = tail[:, i : i + 1], tail[:, half + i : half + i + 1]
+            scale = jnp.where(even, low, high) if mine else jnp.where(even, high, low)
+            keyed = (lin_k[:, lanes(h)].astype(f32) * scale).astype(bf16)
+            state = lax.dot_general(
+                keyed, lin_v[:, lanes(h)], (((0,), (0,)), ((), ())), preferred_element_type=f32
+            )
+            if mine:
+                local[i] = state
+            else:
+                packed[i] = state.astype(bf16)
+                pair_copy(i).start()
+    for held, slot, ahead, ok in kv_beside:
+
+        @pl.when(ok)
+        def _():
+            kv_copy(held, slot, ahead).start()
+
     for d in range(1, window + 1):
 
         @pl.when(me < d)
@@ -397,18 +422,19 @@
         )
         queried[h] = (query.astype(f32) * entry[:, h : h + 1]).astype(bf16)
 
-    for d in (2, 4):
-
-        @pl.when(me >= d)
-        def _():
-            kv_copy(0, d, d).wait_recv()
-
-    for held, slot, ahead, ok in kv_passed:
-
-        @pl.when(ok)
-        def _():
-            kv_copy(held, slot, ahead).start()
-
+    def pass_on(slot_in):
+        @pl.when(me >= slot_in)
+        def _():
+            kv_copy(0, slot_in, slot_in).wait_recv()
+
+        for held, slot, ahead, ok in kv_passed:
+            if held == slot_in:
+
+                @pl.when(ok)
+                def _():
+                    kv_copy(held, slot, ahead).start()
+
+    pass_on(2)
     load(6).wait()
     load(7).wait()
 
@@ -425,7 +451,7 @@
             weights = jnp.exp2((scores - peak) * factor)
             total = jnp.sum(weights, axis=1, keepdims=True)
             numer = jnp.dot(weights.astype(bf16), value_rows, preferred_element_type=f32)
-            soft_out[:, h * width : (h + 1) * width] = (numer / total).astype(bf16)
+            soft_part[:, h * width : (h + 1) * width] = (numer / total).astype(bf16)
 
     def odd_slots():
         for d in (1, 3):
@@ -434,27 +460,43 @@
             def _():
                 kv_copy(0, d, 1).wait_recv()
 
-    z_last = span // 2 - 1
-
-    @pl.when(z == z_last)
-    def _():
-        odd_slots()
-        softmax()
-
     carry_copy().wait_recv()
-    even = x == 0
-    for i in range(half):
+
+    def parts(i):
         h = half * x + i
-        pair_copy(i).wait_recv()
-        own, far = local[h], paired[i].astype(f32)
+        own, far = local[i], paired[i].astype(f32)
         own_carry, far_carry = carries[pl.ds(h, 1), :], carries_in[pl.ds(h, 1), :]
         early, late = jnp.where(even, own, far), jnp.where(even, far, own)
         early_carry = jnp.where(even, own_carry, far_carry)
         late_carry = jnp.where(even, far_carry, own_carry)
+        return early, early_carry, late, late_carry
+
+    for i in range(half):
+        pair_copy(i).wait_recv()
+        early, early_carry, late, late_carry = parts(i)
+        pair = late + late_carry * early
 
         @pl.when(z == 0)
         def _():
+            onward[i] = pair.astype(bf16)
+            chain_copy(i).start()
             arrived[i] = jnp.zeros((width, width), bf16)
+
+        @pl.when(z == 1)
+        def _():
+            ahead_of[i] = pair.astype(bf16)
+            early_copy(i).start()
+
+        @pl.when(z == 2)
+        def _():
+            early_copy(i).wait_recv()
+            before = early_in[i].astype(f32)
+            onward[i] = (pair + (late_carry * early_carry) * before).astype(bf16)
+            chain_copy(i).start()
+
+    pass_on(4)
+    for i in range(half):
+        early, early_carry, late, late_carry = parts(i)
 
         @pl.when(z > 0)
         def _():
@@ -462,20 +504,26 @@
 
         entering_even = arrived[i].astype(f32)
         entering_odd = early + early_carry * entering_even
-        onward[i] = (late + late_carry * entering_odd).astype(bf16)
-
-        @pl.when(me + 2 < span)
-        def _():
+
+        @pl.when(z == 1)
+        def _():
+            onward[i] = (late + late_carry * entering_odd).astype(bf16)
             chain_copy(i).start()
 
-        incoming[h] = jnp.where(even, entering_even, entering_odd).astype(bf16)
         across[i] = jnp.where(even, entering_odd, entering_even).astype(bf16)
         state_copy(i).start()
-
-    @pl.when(z < z_last)
-    def _():
-        odd_slots()
-        softmax()
+        incoming[half * x + i] = jnp.where(even, entering_even, entering_odd).astype(bf16)
+
+    odd_slots()
+    softmax()
+    soft_store = pltpu.make_async_copy(soft_part, soft_out, stores.at[heads])
+    soft_store.start()
+
+    def lin_store(h):
+        columns = pl.ds(h * width, width)
+        return pltpu.make_async_copy(
+            lin_part.at[:, columns], lin_out.at[:, columns], stores.at[h]
+        )
 
     for i in range(half):
         state_copy(i).wait_recv()
@@ -483,7 +531,8 @@
         summed = intra[h] + jnp.dot(queried[h], incoming[h], preferred_element_type=f32)
         mean_square = jnp.mean(summed * summed, axis=1, keepdims=True)
         normed = summed * lax.rsqrt(mean_square + 1e-06) * head(gain, h)
-        lin_out[:, h * width : (h + 1) * width] = normed.astype(bf16)
+        lin_part[:, h * width : (h + 1) * width] = normed.astype(bf16)
+        lin_store(h).start()
 
     carry_copy().wait_send()
     for i in range(half):
@@ -494,11 +543,30 @@
         def _():
             chain_copy(i).wait_send()
 
-    for held, slot, ahead, ok in kv_sent + kv_passed:
+        @pl.when(z == 1)
+        def _():
+            early_copy(i).wait_send()
+
+    for held, slot, ahead, ok in kv_sent + kv_beside + kv_passed:
 
         @pl.when(ok)
         def _():
             kv_copy(held, slot, ahead).wait_send()
+
+    soft_store.wait()
+    for h in range(heads):
+        lin_store(h).wait()
+
+
+def results_kernel(lin_in, soft_in, lin_out, soft_out, sems):
+    copies = [
+        pltpu.make_async_copy(lin_in, lin_out, sems.at[0]),
+        pltpu.make_async_copy(soft_in, soft_out, sems.at[1]),
+    ]
+    for copy in copies:
+        copy.start()
+    for copy in copies:
+        copy.wait()
 
 
 def in_one_kernel(
@@ -518,17 +586,15 @@
     half, window = heads // 2, span // 2
     f32, bf16 = jnp.float32, jnp.bfloat16
     dma = pltpu.SemaphoreType.DMA
-    whole = pl.BlockSpec(memory_space=pltpu.VMEM)
+    far = pl.BlockSpec(memory_space=pltpu.HBM)
     square = (HEAD_DIM, HEAD_DIM)
-    return pl.pallas_call(
+    shapes = (jax.ShapeDtypeStruct((rows, columns), bf16),) * 2
+    lin_out, soft_out = pl.pallas_call(
         functools.partial(block_kernel, span, heads),
-        out_shape=(
-            jax.ShapeDtypeStruct((rows, columns), bf16),
-            jax.ShapeDtypeStruct((rows, columns), bf16),
-        ),
+        out_shape=shapes,
         in_specs=[pl.BlockSpec(memory_space=pltpu.SMEM)]
-        + [pl.BlockSpec(memory_space=pltpu.HBM)] * 8,
-        out_specs=(whole, whole),
+        + [far] * 8,
+        out_specs=(far, far),
         scratch_shapes=[
             pltpu.VMEM((rows, columns), bf16),
             pltpu.VMEM((rows, columns), bf16),
@@ -538,24 +604,31 @@
             pltpu.VMEM((rows, columns), bf16),
             pltpu.VMEM((window + 1, 2, rows, HEAD_DIM), bf16),
             pltpu.VMEM((rows, (window + 1) * rows), f32),
-            pltpu.VMEM((heads, *square), f32),
-            pltpu.VMEM((heads, *square), bf16),
+            pltpu.VMEM((half, *square), f32),
+            pltpu.VMEM((half, *square), bf16),
             pltpu.VMEM((half, *square), bf16),
             pltpu.VMEM((heads, HEAD_DIM), f32),
             pltpu.VMEM((heads, HEAD_DIM), f32),
             pltpu.VMEM((half, *square), bf16),
             pltpu.VMEM((half, *square), bf16),
             pltpu.VMEM((half, *square), bf16),
+            pltpu.VMEM((half, *square), bf16),
+            pltpu.VMEM((half, *square), bf16),
             pltpu.VMEM((heads, *square), bf16),
             pltpu.VMEM((heads, rows, HEAD_DIM), f32),
             pltpu.VMEM((heads, rows, HEAD_DIM), bf16),
+            pltpu.VMEM((rows, columns), bf16),
+            pltpu.VMEM((rows, columns), bf16),
             dma((8,)),
+            dma((heads + 1,)),
             dma((window + 1,)),
             dma((window + 1,)),
             dma((half,)),
             dma((half,)),
             dma,
             dma,
+            dma((half,)),
+            dma((half,)),
             dma((half,)),
             dma((half,)),
             dma((half,)),
@@ -575,6 +648,14 @@
         soft_key,
         soft_value,
     )
+    return pl.pallas_call(
+        results_kernel,
+        out_shape=shapes,
+        in_specs=[far, far],
+        out_specs=(far, far),
+        scratch_shapes=[dma((2,))],
+        compiler_params=pltpu.CompilerParams(vmem_limit_bytes=62 << 20),
+    )(lin_out, soft_out)
 
 
 def solution(mesh):

time: 25 us -> 38.2 us (1.53)
  the two profiles are of different devices: /device:TPU:24 before, /device:TPU:20 now
where the time goes in v3:
time: 38.2 us; the launch traced here: 38 us
  Pallas kernels  37.4 us (98%)
  between operations  0.64 us (2%)
    pallas_call x1, Pallas kernels, in_one_kernel(): pl.pallas_call(functools.partial(block_kernel, span, heads), out_shape=sh...  20.4 us
    pallas_call x1, Pallas kernels, in_one_kernel(): pl.pallas_call(results_kernel, out_shape=shapes, in_specs=[far, far], out...  17 us

profile of v3, /device:TPU:20, one launch (start us, length us, event | category | flops | bytes accessed | tf_op | source)
XLA Modules:
  0.0 38.0 jit_solution(3354667438003921500)
XLA Ops:
  0.6 20.4 %shard_map.104 = (bf16[128,1024]{1,0:T(8,128)(2,1)}, bf16[128,1024]{1,0:T(8,128)(2,1)}) custom-call(s32[1,4]{1,0:T(1,128)} %lens.1, bf16[128,1024]{1,0:T(8,128)(2,1)} %lin_q_far.1, bf16[128,1024]{1,0:T(8,128)(2,1)} %lin_k_far.1, bf16[128,1024]{1,0:T(8,128)(2,1)} %lin_v_far.1, f32[8,128]{1,0:T(8,128)} %bitcast.2, f32[1,1024]{1,0:T(1,128)} %bitcast.3, ...), custom_call_target="tpu_custom_call" | custom-call | tf_op jit(solution)/shard_map/pallas_call | solution.py:592
  21.0 17.0 %shard_map.105 = (bf16[128,1024]{1,0:T(8,128)(2,1)}, bf16[128,1024]{1,0:T(8,128)(2,1)}) custom-call(bf16[128,1024]{1,0:T(8,128)(2,1)} %get-tuple-element.4.lin_in, bf16[128,1024]{1,0:T(8,128)(2,1)} %get-tuple-element.5.soft_in), custom_call_target="tpu_custom_call" | custom-call | tf_op jit(solution)/shard_map/pallas_call | solution.py:651

commit v4 on v3

--- a/solution.py
+++ b/solution.py
@@ -587,6 +587,7 @@
     f32, bf16 = jnp.float32, jnp.bfloat16
     dma = pltpu.SemaphoreType.DMA
     far = pl.BlockSpec(memory_space=pltpu.HBM)
+    near = pl.BlockSpec(memory_space=pltpu.VMEM)
     square = (HEAD_DIM, HEAD_DIM)
     shapes = (jax.ShapeDtypeStruct((rows, columns), bf16),) * 2
     lin_out, soft_out = pl.pallas_call(
@@ -651,10 +652,9 @@
     return pl.pallas_call(
         results_kernel,
         out_shape=shapes,
-        in_specs=[far, far],
+        in_specs=[near, near],
         out_specs=(far, far),
         scratch_shapes=[dma((2,))],
-        compiler_params=pltpu.CompilerParams(vmem_limit_bytes=62 << 20),
     )(lin_out, soft_out)
 
 

time: 38.2 us -> 23 us (0.60)
  Pallas kernels: 37.4 us -> 22.2 us
    pallas_call x1, Pallas kernels: 17 us -> 1.83 us  [in_one_kernel(): pl.pallas_call(results_kernel, out_shape=shapes, in_specs=[near, near], o...]
where the time goes in v4:
time: 23 us; the launch traced here: 22.9 us
  Pallas kernels  22.2 us (97%)
  between operations  0.64 us (3%)
    pallas_call x1, Pallas kernels, in_one_kernel(): pl.pallas_call(functools.partial(block_kernel, span, heads), out_shape=sh...  20.4 us
    pallas_call x1, Pallas kernels, in_one_kernel(): pl.pallas_call(results_kernel, out_shape=shapes, in_specs=[near, near], o...  1.83 us

profile of v4, /device:TPU:20, one launch (start us, length us, event | category | flops | bytes accessed | tf_op | source)
XLA Modules:
  0.0 22.9 jit_solution(1230360449274817509)
XLA Ops:
  0.6 20.4 %shard_map.104 = (bf16[128,1024]{1,0:T(8,128)(2,1)}, bf16[128,1024]{1,0:T(8,128)(2,1)}) custom-call(s32[1,4]{1,0:T(1,128)} %lens.1, bf16[128,1024]{1,0:T(8,128)(2,1)} %lin_q_far.1, bf16[128,1024]{1,0:T(8,128)(2,1)} %lin_k_far.1, bf16[128,1024]{1,0:T(8,128)(2,1)} %lin_v_far.1, f32[8,128]{1,0:T(8,128)} %bitcast.2, f32[1,1024]{1,0:T(1,128)} %bitcast.3, ...), custom_call_target="tpu_custom_call" | custom-call | tf_op jit(solution)/shard_map/pallas_call | solution.py:593
  21.0 1.8 %shard_map.105 = (bf16[128,1024]{1,0:T(8,128)(2,1)}, bf16[128,1024]{1,0:T(8,128)(2,1)}) custom-call(bf16[128,1024]{1,0:T(8,128)(2,1)} %get-tuple-element.4.lin_in, bf16[128,1024]{1,0:T(8,128)(2,1)} %get-tuple-element.5.soft_in), custom_call_target="tpu_custom_call" | custom-call | tf_op jit(solution)/shard_map/pallas_call | solution.py:652

commit v5 on v4

--- a/solution.py
+++ b/solution.py
@@ -196,17 +196,17 @@
     lin_k_far,
     lin_v_far,
     forget_far,
-    gain_far,
     soft_q_far,
     soft_k_far,
     soft_v_far,
-    lin_out,
+    intra_out,
+    queried_out,
+    incoming,
     soft_out,
     lin_q,
     lin_k,
     lin_v,
     forget,
-    gain,
     soft_q,
     pairs,
     bias,
@@ -220,10 +220,9 @@
     early_in,
     ahead_of,
     across,
-    incoming,
+    entered,
     intra,
     queried,
-    lin_part,
     soft_part,
     loads,
     stores,
@@ -259,7 +258,6 @@
             (lin_v_far, lin_v),
             (lin_q_far, lin_q),
             (soft_q_far, soft_q),
-            (gain_far, gain),
         )[i]
         return pltpu.make_async_copy(src, dst, loads.at[i])
 
@@ -275,7 +273,7 @@
         def _():
             pl.semaphore_signal(barrier, inc=1, device_id={"seq": target}, device_id_type=mesh_id)
 
-    for i in range(8):
+    for i in range(7):
         load(i).start()
 
     def remote(src, dst, send, recv, target):
@@ -422,6 +420,16 @@
         )
         queried[h] = (query.astype(f32) * entry[:, h : h + 1]).astype(bf16)
 
+    def part_store(i):
+        src, dst = ((intra, intra_out), (queried, queried_out), (soft_part, soft_out))[i]
+        return pltpu.make_async_copy(src, dst, stores.at[i])
+
+    def entered_store(i):
+        return pltpu.make_async_copy(entered.at[i], incoming.at[half * x + i], stores.at[3 + i])
+
+    part_store(0).start()
+    part_store(1).start()
+
     def pass_on(slot_in):
         @pl.when(me >= slot_in)
         def _():
@@ -436,7 +444,6 @@
 
     pass_on(2)
     load(6).wait()
-    load(7).wait()
 
     def softmax():
         key_rows = pairs[:, 0].reshape((window + 1) * rows, width)
@@ -512,28 +519,14 @@
 
         across[i] = jnp.where(even, entering_odd, entering_even).astype(bf16)
         state_copy(i).start()
-        incoming[half * x + i] = jnp.where(even, entering_even, entering_odd).astype(bf16)
+        entered[i] = jnp.where(even, entering_even, entering_odd).astype(bf16)
+        entered_store(i).start()
 
     odd_slots()
     softmax()
-    soft_store = pltpu.make_async_copy(soft_part, soft_out, stores.at[heads])
-    soft_store.start()
-
-    def lin_store(h):
-        columns = pl.ds(h * width, width)
-        return pltpu.make_async_copy(
-            lin_part.at[:, columns], lin_out.at[:, columns], stores.at[h]
-        )
-
+    part_store(2).start()
     for i in range(half):
         state_copy(i).wait_recv()
-    for h in range(heads):
-        summed = intra[h] + jnp.dot(queried[h], incoming[h], preferred_element_type=f32)
-        mean_square = jnp.mean(summed * summed, axis=1, keepdims=True)
-        normed = summed * lax.rsqrt(mean_square + 1e-06) * head(gain, h)
-        lin_part[:, h * width : (h + 1) * width] = normed.astype(bf16)
-        lin_store(h).start()
-
     carry_copy().wait_send()
     for i in range(half):
         pair_copy(i).wait_send()
@@ -553,20 +546,46 @@
         def _():
             kv_copy(held, slot, ahead).wait_send()
 
+    for i in range(3):
+        part_store(i).wait()
+    for i in range(half):
+        entered_store(i).wait()
+
+
+def finish_kernel(
+    heads, intra_far, queried_far, incoming_far, soft_far, gain, lin_out, soft_out,
+    intra, queried, incoming, soft, lin, loads, stores,
+):
+    width = HEAD_DIM
+
+    def load(i, h):
+        src, dst = ((intra_far, intra), (queried_far, queried), (incoming_far, incoming))[i]
+        return pltpu.make_async_copy(src.at[h], dst.at[h], loads.at[3 * h + i])
+
+    def lin_store(h):
+        columns = pl.ds(h * width, width)
+        return pltpu.make_async_copy(lin.at[:, columns], lin_out.at[:, columns], stores.at[h])
+
+    soft_load = pltpu.make_async_copy(soft_far, soft, loads.at[3 * heads])
+    soft_store = pltpu.make_async_copy(soft, soft_out, stores.at[heads])
+    soft_load.start()
+    for h in range(heads):
+        for i in range(3):
+            load(i, h).start()
+    soft_load.wait()
+    soft_store.start()
+    for h in range(heads):
+        for i in range(3):
+            load(i, h).wait()
+        summed = intra[h] + jnp.dot(queried[h], incoming[h], preferred_element_type=jnp.float32)
+        mean_square = jnp.mean(summed * summed, axis=1, keepdims=True)
+        columns = slice(h * width, (h + 1) * width)
+        normed = summed * lax.rsqrt(mean_square + 1e-06) * gain[:, columns]
+        lin[:, columns] = normed.astype(jnp.bfloat16)
+        lin_store(h).start()
     soft_store.wait()
     for h in range(heads):
         lin_store(h).wait()
-
-
-def results_kernel(lin_in, soft_in, lin_out, soft_out, sems):
-    copies = [
-        pltpu.make_async_copy(lin_in, lin_out, sems.at[0]),
-        pltpu.make_async_copy(soft_in, soft_out, sems.at[1]),
-    ]
-    for copy in copies:
-        copy.start()
-    for copy in copies:
-        copy.wait()
 
 
 def in_one_kernel(
@@ -589,19 +608,20 @@
     far = pl.BlockSpec(memory_space=pltpu.HBM)
     near = pl.BlockSpec(memory_space=pltpu.VMEM)
     square = (HEAD_DIM, HEAD_DIM)
-    shapes = (jax.ShapeDtypeStruct((rows, columns), bf16),) * 2
-    lin_out, soft_out = pl.pallas_call(
+    shape = jax.ShapeDtypeStruct
+    states = (heads, *square)
+    parts = (shape(states, f32), shape(states, bf16), shape(states, bf16), shape((rows, columns), bf16))
+    parts = pl.pallas_call(
         functools.partial(block_kernel, span, heads),
-        out_shape=shapes,
+        out_shape=parts,
         in_specs=[pl.BlockSpec(memory_space=pltpu.SMEM)]
-        + [far] * 8,
-        out_specs=(far, far),
+        + [far] * 7,
+        out_specs=(far,) * 4,
         scratch_shapes=[
             pltpu.VMEM((rows, columns), bf16),
             pltpu.VMEM((rows, columns), bf16),
             pltpu.VMEM((rows, columns), bf16),
             pltpu.VMEM((heads, rows), f32),
-            pltpu.VMEM((1, columns), f32),
             pltpu.VMEM((rows, columns), bf16),
             pltpu.VMEM((window + 1, 2, rows, HEAD_DIM), bf16),
             pltpu.VMEM((rows, (window + 1) * rows), f32),
@@ -615,13 +635,12 @@
             pltpu.VMEM((half, *square), bf16),
             pltpu.VMEM((half, *square), bf16),
             pltpu.VMEM((half, *square), bf16),
-            pltpu.VMEM((heads, *square), bf16),
+            pltpu.VMEM((half, *square), bf16),
             pltpu.VMEM((heads, rows, HEAD_DIM), f32),
             pltpu.VMEM((heads, rows, HEAD_DIM), bf16),
             pltpu.VMEM((rows, columns), bf16),
-            pltpu.VMEM((rows, columns), bf16),
-            dma((8,)),
-            dma((heads + 1,)),
+            dma((7,)),
+            dma((3 + half,)),
             dma((window + 1,)),
             dma((window + 1,)),
             dma((half,)),
@@ -644,18 +663,26 @@
         lin_key,
         lin_value,
         forget_log.T,
-        norm_gain.reshape(1, columns),
         soft_query,
         soft_key,
         soft_value,
     )
     return pl.pallas_call(
-        results_kernel,
-        out_shape=shapes,
-        in_specs=[near, near],
+        functools.partial(finish_kernel, heads),
+        out_shape=(shape((rows, columns), bf16),) * 2,
+        in_specs=[far] * 4 + [near],
         out_specs=(far, far),
-        scratch_shapes=[dma((2,))],
-    )(lin_out, soft_out)
+        scratch_shapes=[
+            pltpu.VMEM(states, f32),
+            pltpu.VMEM(states, bf16),
+            pltpu.VMEM(states, bf16),
+            pltpu.VMEM((rows, columns), bf16),
+            pltpu.VMEM((rows, columns), bf16),
+            dma((3 * heads + 1,)),
+            dma((heads + 1,)),
+        ],
+        compiler_params=pltpu.CompilerParams(vmem_limit_bytes=62 << 20),
+    )(*parts, norm_gain.reshape(1, columns))
 
 
 def solution(mesh):

time: 23 us -> 25.4 us (1.10)
  Pallas kernels: 22.2 us -> 24.6 us
    pallas_call x2, Pallas kernels: 22.2 us -> 24.6 us  [the longest x1 20.1 us: in_one_kernel(): pl.pallas_call(functools.partial(block_kernel, span, heads), out_shape=pa...]
where the time goes in v5:
time: 25.4 us; the launch traced here: 25.2 us
  Pallas kernels  24.6 us (97%)
  between operations  0.64 us (3%)
    pallas_call x1, Pallas kernels, in_one_kernel(): pl.pallas_call(functools.partial(block_kernel, span, heads), out_shape=pa...  20.1 us
    pallas_call x1, Pallas kernels, in_one_kernel(): pl.pallas_call(functools.partial(finish_kernel, heads), out_shape=(shape(...  4.48 us

profile of v5, /device:TPU:20, one launch (start us, length us, event | category | flops | bytes accessed | tf_op | source)
XLA Modules:
  0.0 25.2 jit_solution(7947111566193149994)
XLA Ops:
  0.6 20.1 %shard_map.104 = (f32[8,128,128]{2,1,0:T(8,128)}, bf16[8,128,128]{2,1,0:T(8,128)(2,1)}, bf16[8,128,128]{2,1,0:T(8,128)(2,1)}, bf16[128,1024]{1,0:T(8,128)(2,1)}) custom-call(s32[1,4]{1,0:T(1,128)} %lens.1, bf16[128,1024]{1,0:T(8,128)(2,1)} %lin_q_far.1, bf16[128,1024]{1,0:T(8,128)(2,1)} %lin_k_far.1, bf16[128,1024]{1,0:T(8,128)(2,1)} %lin_v_far.1, ...), custom_call_target="tpu_custom_call" | custom-call | tf_op jit(solution)/shard_map/pallas_call | solution.py:614
  20.7 4.5 %shard_map.105 = (bf16[128,1024]{1,0:T(8,128)(2,1)}, bf16[128,1024]{1,0:T(8,128)(2,1)}) custom-call(f32[8,128,128]{2,1,0:T(8,128)} %get-tuple-element.6.intra_far, bf16[8,128,128]{2,1,0:T(8,128)(2,1)} %get-tuple-element.7.queried_far, bf16[8,128,128]{2,1,0:T(8,128)(2,1)} %get-tuple-element.8.incoming_far, bf16[128,1024]{1,0:T(8,128)(2,1)} %get-tuple-element.9.soft_far, ...), custom_call_target="tpu_custom_call" | custom-call | tf_op jit(solution)/shard_map/pallas_call | solution.py:670
